TPU v7x, 512 devices: a whole 4x4x16 slice. The times are simulated.
512 devices in a mesh: gx: 16 (over z), gy: 32 (over y, x, core).
Axes of the slice: x: 4, y: 4, z: 16, core: 2. Of those that a mesh axis runs over, the one named last changes fastest.
Arguments:
- adjoint_guess: float32 [64, 512, 256], P('gx', 'gy'), may hold values from -80 to 80, as said below
- velocity: float32 [3, 64, 16384], P(None, 'gx', 'gy'), may hold values from -1 to 1
- leaf_rate: float32 [64, 16384], P('gx', 'gy'), may hold values from 0.2 to 5
- canopy: int32 [64, 16384], P('gx', 'gy'), may hold values from 0 to 1, as said below
- solid: int32 [64, 16384], P('gx', 'gy'), may hold values from 0 to 1, as said below
- receptors: int32 [8], replicated, may hold values from 0 to 32767
Outputs:
- adjoint_field: float32 [64, 512, 256], P('gx', 'gy')
- residual: float32 [64, 512, 256], P('gx', 'gy')
Inputs may be any that keep to these rules, and one draw needn't show every extreme that they name: `adjoint_guess`: finite values. 1 marks building cells; every horizontal column is solid from the ground up to its building's height. `canopy`: 1 marks tree-crown cells; none is solid.
All inputs are finite; a program needn't handle non-finite values.
Results may differ from a plain program's by a relative error of at most 0.0003.
Values sent between devices are 32-bit elements; how exact they have to be, the bound alone decides.
A program may use at most 64 MiB of HBM per device.

v0:
```python
import jax
import jax.numpy as jnp
from jax import lax
from jax.sharding import PartitionSpec as P

NZ = 32
R = 8
CYCLES = 3


horiz_diff = 4.0
vert_diff = 2.0
decay_rate = 3.5
penalty = 40.0
leaf_gain = 4.0
source_gain = 32.0


def padded_2(shard, sides, width):
    for axis, dim in sides:
        size, length = (lax.axis_size(axis), shard.shape[dim])
        up = [(i, (i + 1) % size) for i in range(size - 1)]
        down = [(j, i) for i, j in up]
        last = lax.slice_in_dim(shard, length - width, length, axis=dim)
        initial = lax.slice_in_dim(shard, 0, width, axis=dim)
        before = lax.ppermute(last, axis, up)
        after = lax.ppermute(initial, axis, down)
        shard = jnp.concatenate([before, shard, after], axis=dim)
    return shard


def coefficient_fields(flows, reaction):
    east_flow = flows[0]
    north_flow = flows[1]
    rise_flow = flows[2]
    couplings = [
        horiz_diff + jax.nn.relu(east_flow),
        horiz_diff + jax.nn.relu(-east_flow),
        horiz_diff + jax.nn.relu(north_flow),
        horiz_diff + jax.nn.relu(-north_flow),
        vert_diff + jax.nn.relu(rise_flow),
        vert_diff + jax.nn.relu(-rise_flow),
    ]
    diagonal = (
        decay_rate
        + reaction
        + couplings[0]
        + couplings[1]
        + couplings[2]
        + couplings[3]
        + couplings[4]
        + couplings[5]
    )
    return [jnp.repeat(piece, R, axis=-1) for piece in [diagonal] + couplings]


def apply_operator(padded, coefficients):
    centre = padded[1:-1, 1:-1]
    zero_lane = jnp.zeros(centre.shape[:-1] + (R,), jnp.float32)
    upper_cells = jnp.concatenate([centre[..., R:], zero_lane], axis=-1)
    lower_cells = jnp.concatenate([zero_lane, centre[..., :-R]], axis=-1)
    diagonal, east_c, west_c, north_c, south_c, upper_c, lower_c = coefficients
    return (
        diagonal * centre
        - east_c * padded[2:, 1:-1]
        - west_c * padded[:-2, 1:-1]
        - north_c * padded[1:-1, 2:]
        - south_c * padded[1:-1, :-2]
        - upper_c * upper_cells
        - lower_c * lower_cells
    )


def per_receptor(first, second):
    return jnp.sum((first * second).reshape(-1, R), axis=0)


def spread_lanes(values):
    return jnp.tile(values, NZ)


def residual_of(image_in, source_in):
    return source_in - image_in


def body(adjoint_guess, velocity, leaf_rate, canopy, solid, receptors):
    rows_dev = adjoint_guess.shape[0]
    cols_dev = adjoint_guess.shape[1]
    total_cols = cols_dev * lax.axis_size("gy")
    row_start = lax.axis_index("gx") * rows_dev
    col_start = lax.axis_index("gy") * cols_dev
    flows = velocity.reshape(3, rows_dev, cols_dev, NZ)
    reaction = (
        penalty * solid.astype(jnp.float32) + leaf_gain * leaf_rate * canopy.astype(jnp.float32)
    ).reshape(rows_dev, cols_dev, NZ)
    coefficients = coefficient_fields(flows, reaction)
    rec_rows = receptors // total_cols
    rec_cols = receptors % total_cols

    def operate(values):
        padded = padded_2(values, (("gx", 0), ("gy", 1)), 1)
        return apply_operator(padded, coefficients)

    global_rows = row_start + jnp.arange(rows_dev, dtype=jnp.int32)
    global_cols = col_start + jnp.arange(cols_dev, dtype=jnp.int32)
    hit_rows = (global_rows[:, None] == rec_rows[None, :]).astype(jnp.float32)
    hit_cols = (global_cols[:, None] == rec_cols[None, :]).astype(jnp.float32)
    receptor_plane = source_gain * hit_rows[:, None, :] * hit_cols[None, :, :]
    ground_lane = jnp.zeros((rows_dev, cols_dev, R), jnp.float32)
    upper_lanes = jnp.zeros((rows_dev, cols_dev, (NZ - 2) * R), jnp.float32)
    source = jnp.concatenate([ground_lane, receptor_plane, upper_lanes], axis=-1)
    iterate = adjoint_guess
    first_image = operate(iterate)
    middle = residual_of(first_image, source)
    second_image = operate(middle)
    residual = middle
    image_dir = second_image
    for cycle_index in range(CYCLES):
        if cycle_index > 0:
            image_dir = operate(residual)
        squares, against = lax.psum(
            (per_receptor(residual, residual), per_receptor(residual, image_dir)), ("gx", "gy")
        )
        alpha_step = squares / against
        halfway = residual - spread_lanes(alpha_step) * image_dir
        turned = operate(halfway)
        along_turn, turn_power = lax.psum(
            (per_receptor(turned, halfway), per_receptor(turned, turned)), ("gx", "gy")
        )
        omega_step = along_turn / turn_power
        iterate = iterate + spread_lanes(alpha_step) * residual + spread_lanes(omega_step) * halfway
        residual = halfway - spread_lanes(omega_step) * turned
    return (iterate, residual)


def solution(mesh):
    return jax.shard_map(
        body,
        mesh=mesh,
        in_specs=(
            P("gx", "gy", None),
            P(None, "gx", "gy"),
            P("gx", "gy"),
            P("gx", "gy"),
            P("gx", "gy"),
            P(),
        ),
        out_specs=(P("gx", "gy", None), P("gx", "gy", None)),
        check_vma=False,
    )
```

profile of v0, /device:TPU:1, one launch (start us, length us, event | category | flops | bytes accessed | tf_op | source)
XLA Modules:
  0.0 755.6 jit_solution(6809923909416197719)
XLA Ops:
  0.6 1.4 fusion.100
  2.0 1.3 collective-permute-start
  3.3 5.6 collective-permute-start.1
  8.9 0.7 fusion.101
  9.7 0.6 iota_add_fusion.1
  11.5 0.6 copy-done.4
  13.5 0.8 broadcast_bitcast_fusion.5
  14.4 0.7 copy-done.10
  15.1 0.7 copy-done.12
  15.8 0.7 constant_dynamic-update-slice_fusion.2
  16.6 0.6 fusion.87
  17.2 8.3 %collective-permute-start.2 = (f32[6,1,256]{2,1,0:T(1,128)}, f32[6,1,256]{2,1,0:T(1,128)}, u32[]{:S(2)}, u32[]{:S(2)}) collective-permute-start(f32[6,1,256]{2,1,0:T(1,128)} %get-tuple-element.50), channel_id=1, source_target_pairs={{1,0},{2,1},{3,2},{4,3},{5,4},{6,5},{7,6},{8,7},{9,8},{10,9},{11,1... | collective-permute-start | bytes 18440 | tf_op jit(solution)/shard_map/ppermute | solution.py:27
  25.5 1.9 collective-permute-start.3
  28.0 0.6 pad.114.clone
  29.7 0.7 copy-done
  30.6 0.6 copy-done.2
  31.3 0.8 fusion.85
  32.1 1.3 collective-permute-start.5
  33.4 1.3 collective-permute-start.4
  34.7 3.2 collective-permute-done.4
  37.9 4.2 collective-permute-start.6
  42.1 1.9 collective-permute-start.7
  44.1 0.6 reshape.179
  45.3 0.6 reshape.180
  46.1 111.9 %all-reduce.19 = (f32[8]{0:T(128)S(1)}, f32[8]{0:T(128)S(1)}) all-reduce(f32[8]{0:T(128)S(1)} %reduce_sum.108, f32[8]{0:T(128)S(1)} %reduce_sum.109), channel_id=1, replica_groups=mesh['gx'=16,'gy'=32] {'gx','gy'}, use_global_device_ids=true, to_apply=%region_1.2 | all-reduce | flops 16 | bytes 128 | tf_op jit(solution)/shard_map/psum | solution.py:121
  158.2 1.3 collective-permute-start.9
  159.5 1.3 collective-permute-start.8
  160.8 3.2 collective-permute-done.8
  164.0 4.1 collective-permute-start.10
  168.2 1.9 collective-permute-start.11
  170.2 1.0 collective-permute-done.11
  172.2 0.6 reshape.182
  173.1 104.2 %all-reduce.18 = (f32[8]{0:T(128)S(1)}, f32[8]{0:T(128)S(1)}) all-reduce(f32[8]{0:T(128)S(1)} %reduce_sum.110, f32[8]{0:T(128)S(1)} %reduce_sum.111), channel_id=1, replica_groups=mesh['gx'=16,'gy'=32] {'gx','gy'}, use_global_device_ids=true, to_apply=%region_5.6 | all-reduce | flops 16 | bytes 128 | tf_op jit(solution)/shard_map/psum | solution.py:127
  277.4 1.3 collective-permute-start.13
  278.7 1.3 collective-permute-start.12
  280.0 3.2 collective-permute-done.12
  283.2 3.7 collective-permute-start.14
  286.9 1.9 collective-permute-start.15
  288.9 0.6 reshape.183
  290.9 105.5 %all-reduce.17 = (f32[8]{0:T(128)S(1)}, f32[8]{0:T(128)S(1)}) all-reduce(f32[8]{0:T(128)S(1)} %reduce_sum.112, f32[8]{0:T(128)S(1)} %reduce_sum.113), channel_id=1, replica_groups=mesh['gx'=16,'gy'=32] {'gx','gy'}, use_global_device_ids=true, to_apply=%region_9.10 | all-reduce | flops 16 | bytes 128 | tf_op jit(solution)/shard_map/psum | solution.py:121
  396.5 1.3 collective-permute-start.17
  397.8 1.3 collective-permute-start.16
  399.1 3.2 collective-permute-done.16
  402.3 4.0 collective-permute-start.18
  406.4 1.9 collective-permute-start.19
  408.4 1.0 collective-permute-done.19
  410.4 0.6 reshape.186
  411.3 104.9 %all-reduce.16 = (f32[8]{0:T(128)S(1)}, f32[8]{0:T(128)S(1)}) all-reduce(f32[8]{0:T(128)S(1)} %reduce_sum.114, f32[8]{0:T(128)S(1)} %reduce_sum.115), channel_id=1, replica_groups=mesh['gx'=16,'gy'=32] {'gx','gy'}, use_global_device_ids=true, to_apply=%region_13.14 | all-reduce | flops 16 | bytes 128 | tf_op jit(solution)/shard_map/psum | solution.py:127
  516.3 1.3 collective-permute-start.21
  517.6 1.3 collective-permute-start.20
  518.9 3.2 collective-permute-done.20
  522.1 4.0 collective-permute-start.22
  526.1 2.1 collective-permute-start.23
  528.3 0.6 reshape.187
  530.2 104.8 %all-reduce.15 = (f32[8]{0:T(128)S(1)}, f32[8]{0:T(128)S(1)}) all-reduce(f32[8]{0:T(128)S(1)} %reduce_sum.116, f32[8]{0:T(128)S(1)} %reduce_sum.117), channel_id=1, replica_groups=mesh['gx'=16,'gy'=32] {'gx','gy'}, use_global_device_ids=true, to_apply=%region_17.18 | all-reduce | flops 16 | bytes 128 | tf_op jit(solution)/shard_map/psum | solution.py:121
  635.2 1.3 collective-permute-start.25
  636.4 1.3 collective-permute-start.24
  637.8 3.2 collective-permute-done.24
  640.9 4.0 collective-permute-start.26
  645.0 1.9 collective-permute-start.27
  647.0 1.0 collective-permute-done.27
  649.0 0.6 reshape.190
  649.9 104.9 %all-reduce.14 = (f32[8]{0:T(128)S(1)}, f32[8]{0:T(128)S(1)}) all-reduce(f32[8]{0:T(128)S(1)} %reduce_sum.118, f32[8]{0:T(128)S(1)} %reduce_sum.119), channel_id=1, replica_groups=mesh['gx'=16,'gy'=32] {'gx','gy'}, use_global_device_ids=true, to_apply=%region_21.22 | all-reduce | flops 16 | bytes 128 | tf_op jit(solution)/shard_map/psum | solution.py:127
  754.9 0.7 multiply_subtract_fusion
  (151 shorter events, 13.0 us)
Async XLA Ops:
  0.6 8.3 %copy-start.1 = (f32[4,16,256]{2,1,0:T(8,128)S(1)}, f32[4,16,256]{2,1,0:T(8,128)}, u32[]{:S(2)}) copy-start(f32[4,16,256]{2,1,0:T(8,128)} %param.6) | copy-start | bytes 196612
  2.0 14.5 %collective-permute-start = (f32[1,16,256]{2,1,0:T(8,128)}, f32[1,16,256]{2,1,0:T(8,128)S(1)}, u32[]{:S(2)}, u32[]{:S(2)}) collective-permute-start(f32[1,16,256]{2,1,0:T(8,128)} %get-tuple-element.78), channel_id=1, source_target_pairs={{32,0},{64,32},{96,64},{128,96},{160,128},{192,160},{224,192},{256... | collective-permute-start | bytes 49160 | tf_op jit(solution)/shard_map/ppermute | solution.py:27
  3.3 12.5 %collective-permute-start.1 = (f32[1,16,256]{2,1,0:T(8,128)}, f32[1,16,256]{2,1,0:T(8,128)}, u32[]{:S(2)}, u32[]{:S(2)}) collective-permute-start(f32[1,16,256]{2,1,0:T(8,128)} %get-tuple-element.79), channel_id=1, source_target_pairs={{0,32},{32,64},{64,96},{96,128},{128,160},{160,192},{192,224},{224... | collective-permute-start | bytes 49160 | tf_op jit(solution)/shard_map/ppermute | solution.py:26
  8.9 2.5 copy-start.7
  9.6 1.2 copy-start.14
  9.6 1.7 copy-start.6
  9.6 1.7 copy-start.5
  11.4 0.7 copy-start.4
  14.4 0.7 copy-start.10
  14.4 0.7 copy-start.11
  15.1 0.7 copy-start.12
  15.1 0.7 copy-start.13
  17.2 13.4 %collective-permute-start.2 = (f32[6,1,256]{2,1,0:T(1,128)}, f32[6,1,256]{2,1,0:T(1,128)}, u32[]{:S(2)}, u32[]{:S(2)}) collective-permute-start(f32[6,1,256]{2,1,0:T(1,128)} %get-tuple-element.50), channel_id=1, source_target_pairs={{1,0},{2,1},{3,2},{4,3},{5,4},{6,5},{7,6},{8,7},{9,8},{10,9},{11,1... | collective-permute-start | bytes 18440 | tf_op jit(solution)/shard_map/ppermute | solution.py:27
  25.5 5.1 collective-permute-start.3
  29.4 1.1 copy-start
  30.4 0.8 copy-start.2
  30.4 0.9 copy-start.3
  30.4 0.9 copy-start.9
  30.6 0.7 copy-start.8
  32.1 2.6 collective-permute-start.5
  33.4 4.5 collective-permute-start.4
  37.9 7.1 collective-permute-start.6
  42.1 3.1 collective-permute-start.7
  158.2 2.6 collective-permute-start.9
  159.5 4.5 collective-permute-start.8
  164.0 6.2 collective-permute-start.10
  168.2 3.1 collective-permute-start.11
  277.4 2.6 collective-permute-start.13
  278.7 4.5 collective-permute-start.12
  283.2 6.6 collective-permute-start.14
  286.9 3.1 collective-permute-start.15
  396.5 2.6 collective-permute-start.17
  397.8 4.5 collective-permute-start.16
  402.3 6.0 collective-permute-start.18
  406.4 3.1 collective-permute-start.19
  516.3 2.6 collective-permute-start.21
  517.6 4.5 collective-permute-start.20
  522.1 7.1 collective-permute-start.22
  526.1 3.1 collective-permute-start.23
  635.2 2.6 collective-permute-start.25
  636.4 4.5 collective-permute-start.24
  640.9 6.0 collective-permute-start.26
  645.0 3.1 collective-permute-start.27
where the time goes:
time: 758 us; the launch traced here: 756 us
  blocking collectives  636 us (84%)
  starting transfers between devices  68.4 us (9%)
  waiting for transfers between devices  22.6 us (3%)
  local copies, waits for them, and re-layouts  19.5 us (3%)
  other arithmetic  7.63 us (1%)
    psum x3, blocking collectives, body(): lax.psum((per_receptor(residual, residual), per_receptor(residual, image_...  322 us
    psum x3, blocking collectives, body(): lax.psum((per_receptor(turned, halfway), per_receptor(turned, turned)), (...  314 us
    ppermute x14, starting transfers between devices, padded_2(): after = lax.ppermute(initial, axis, down)  41.4 us
    ppermute x14, starting transfers between devices, padded_2(): before = lax.ppermute(last, axis, up)  27 us
    ppermute x14, waiting for transfers between devices, padded_2(): after = lax.ppermute(initial, axis, down)  19.1 us
  transfers between devices with their start and end apart: 28, of which 11 were waited for; matrix products, arithmetic and copies ran while one was open for 1% of the time, Pallas kernels for 0%

commit v1 on v0

v1 whole, which is shorter than its diff:
```python
import functools

import jax
import jax.numpy as jnp
from jax import lax
from jax.experimental import pallas as pl
from jax.experimental.pallas import tpu as pltpu
from jax.sharding import PartitionSpec as P

NZ = 32
R = 8
CYCLES = 3
DEGREE = 2 * CYCLES

horiz_diff = 4.0
vert_diff = 2.0
decay_rate = 3.5
penalty = 40.0
leaf_gain = 4.0
source_gain = 32.0

SHIFT = 46.5
SCALE = 32.0

PAD_R = 4
PAD_C = 8
LANES = 128

PAIRS = [(a, b) for a in range(DEGREE + 1) for b in range(a + 1)]
SLOT = {pair: n for n, pair in enumerate(PAIRS)}
SIDES = [(dx, dy) for dx in (1, -1, 0) for dy in (0, 1, -1) if (dx, dy) != (0, 0)]


def window(delta, reach, own, pad):
    if delta == 0:
        return pl.ds(pad, own), pl.ds(pad, own)
    if delta > 0:
        return pl.ds(pad + own - reach, reach), pl.ds(pad - reach, reach)
    return pl.ds(pad, reach), pl.ds(pad + own, reach)


def kernel(
    nx, ny, rows, cols,
    guess, velocity, leaf, canopy, solid, receptors,
    field_out, residual_out,
    start, basis, packed, coef, raw_vel, raw_leaf, raw_canopy, raw_solid,
    gram, mine, plane_in, line, line_in,
    load_sem, halo_send, halo_recv, plane_send, plane_recv, line_send, line_recv,
):
    gx = lax.axis_index("gx")
    gy = lax.axis_index("gy")

    def peer(dx, dy):
        return {
            "gx": lax.rem(gx + dx + nx, nx) if dx else gx,
            "gy": lax.rem(gy + dy + ny, ny) if dy else gy,
        }

    barrier = pltpu.get_barrier_semaphore()
    greeted = [(0, d) for d in range(1, ny)] + [(d, 0) for d in range(1, nx)]
    greeted += [side for side in SIDES if side[0] and side[1]]
    for side in greeted:
        pl.semaphore_signal(barrier, inc=1, device_id=peer(*side), device_id_type=pl.DeviceIdType.MESH)

    own_r, own_c = pl.ds(PAD_R, rows), pl.ds(PAD_C, cols)
    loads = [
        pltpu.make_async_copy(velocity, raw_vel, load_sem.at[0]),
        pltpu.make_async_copy(leaf, raw_leaf, load_sem.at[1]),
        pltpu.make_async_copy(canopy, raw_canopy, load_sem.at[2]),
        pltpu.make_async_copy(solid, raw_solid, load_sem.at[3]),
        pltpu.make_async_copy(guess, start.at[own_r, own_c], load_sem.at[4]),
    ]
    for copy in loads:
        copy.start()

    sub = lax.broadcasted_iota(jnp.int32, (8, LANES), 0)
    lane = lax.broadcasted_iota(jnp.int32, (8, LANES), 1)

    for copy in loads[:4]:
        copy.wait()
    reaction = penalty * raw_solid[...].astype(jnp.float32) + leaf_gain * raw_leaf[...] * raw_canopy[...].astype(jnp.float32)
    parts = [raw_vel[0], raw_vel[1], raw_vel[2], reaction]
    spread = (sub % 4) * NZ + lane % NZ
    for i in range(rows):
        for tile in range(cols // 8):
            total = None
            for n, part in enumerate(parts):
                low = jnp.broadcast_to(part[i : i + 1, (2 * tile) * LANES : (2 * tile + 1) * LANES], (8, LANES))
                high = jnp.broadcast_to(part[i : i + 1, (2 * tile + 1) * LANES : (2 * tile + 2) * LANES], (8, LANES))
                value = jnp.take_along_axis(jnp.where(sub < 4, low, high), spread, axis=1)
                total = value if total is None else jnp.where(lane // NZ == n, value, total)
            packed[PAD_R + i, PAD_C + 8 * tile : PAD_C + 8 * tile + 8, :] = total

    loads[4].wait()
    pl.semaphore_wait(barrier, len(greeted))

    def exchange(ref, bank, reach):
        copies = []
        for n, (dx, dy) in enumerate(SIDES):
            near = reach - 1 if dx and dy else reach
            src_r, dst_r = window(dx, near, rows, PAD_R)
            src_c, dst_c = window(dy, near, cols, PAD_C)
            copies.append(
                pltpu.make_async_remote_copy(
                    src_ref=ref.at[src_r, src_c],
                    dst_ref=ref.at[dst_r, dst_c],
                    send_sem=halo_send.at[bank, n],
                    recv_sem=halo_recv.at[bank, n],
                    device_id=peer(dx, dy),
                    device_id_type=pl.DeviceIdType.MESH,
                )
            )
        for copy in copies:
            copy.start()
        return copies

    moving = exchange(packed, 0, 3) + exchange(start, 1, 4)
    for copy in moving:
        copy.wait_recv()

    inv = 1.0 / SCALE
    first_row = jnp.where(gx == 0, 0.0, inv)
    last_row = jnp.where(gx == nx - 1, 0.0, inv)
    first_col = jnp.where(gy == 0, 0.0, inv)
    last_col = jnp.where(gy == ny - 1, 0.0, inv)
    tiles = (cols + 2 * PAD_C) // 8
    first_tile, last_tile = PAD_C // 8, (PAD_C + cols) // 8 - 1
    for r in range(PAD_R - 3, PAD_R + rows + 3):
        outer = r in (PAD_R - 3, PAD_R + rows + 2)
        for tile in range(first_tile, last_tile + 1) if outer else range(tiles):
            here = pl.ds(8 * tile, 8)
            cell = packed[r, 8 * tile : 8 * tile + 8, :]
            for half in range(2):
                span = slice(half * LANES, (half + 1) * LANES)
                level = lane // R + half * (LANES // R)
                u, v, w, react = (jnp.take_along_axis(cell, n * NZ + level, axis=1) for n in range(4))
                relu = lambda value: jnp.maximum(value, 0.0)
                east, west = horiz_diff + relu(u), horiz_diff + relu(-u)
                north, south = horiz_diff + relu(v), horiz_diff + relu(-v)
                up, down = vert_diff + relu(w), vert_diff + relu(-w)
                diag = decay_rate + react + east + west + north + south + up + down
                coef[0, r, here, span] = (diag - SHIFT) * inv
                coef[1, r, here, span] = east * (last_row if r == PAD_R + rows - 1 else inv)
                coef[2, r, here, span] = west * (first_row if r == PAD_R else inv)
                coef[3, r, here, span] = north * (jnp.where(sub == 7, last_col, inv) if tile == last_tile else inv)
                coef[4, r, here, span] = south * (jnp.where(sub == 0, first_col, inv) if tile == first_tile else inv)
                coef[5, r, here, span] = up * (jnp.where(lane >= LANES - R, 0.0, inv) if half else inv)
                coef[6, r, here, span] = down * (inv if half else jnp.where(lane < R, 0.0, inv))

    def apply(ref, r, inner):
        height = cols + 2 * PAD_C
        width = NZ * R
        cut = slice(PAD_C, PAD_C + cols) if inner else slice(0, height)
        centre = ref[r]
        north = pltpu.roll(centre, height - 1, 0)[cut]
        south = pltpu.roll(centre, 1, 0)[cut]
        middle = centre[cut]
        up = pltpu.roll(middle, width - R, 1)
        down = pltpu.roll(middle, R, 1)
        return (
            coef[0, r, cut, :] * middle
            - coef[1, r, cut, :] * ref[r + 1, cut, :]
            - coef[2, r, cut, :] * ref[r - 1, cut, :]
            - coef[3, r, cut, :] * north
            - coef[4, r, cut, :] * south
            - coef[5, r, cut, :] * up
            - coef[6, r, cut, :] * down
        )

    height = cols + 2 * PAD_C
    lanes = lax.broadcasted_iota(jnp.int32, (height, NZ * R), 1)
    place = lax.broadcasted_iota(jnp.int32, (height, NZ * R), 0) + (gy * cols - PAD_C)
    aim = jnp.full((height, NZ * R), -1 << 30, jnp.int32)
    for q in range(R):
        aim = jnp.where(lanes == R + q, receptors[q], aim)
    aim = aim - place
    for r in range(PAD_R - 3, PAD_R + rows + 3):
        source = jnp.where(aim == (gx * rows + (r - PAD_R)) * (ny * cols), source_gain, 0.0)
        basis[0, r] = source - (SCALE * apply(start, r, False) + SHIFT * start[r])

    def advance(j, reach):
        for r in range(PAD_R - reach, PAD_R + rows + reach):
            if reach:
                basis[j, r] = apply(basis.at[j - 1], r, False)
            else:
                basis[j, r, PAD_C : PAD_C + cols, :] = apply(basis.at[j - 1], r, True)

    def products(pairs):
        sums = {}
        for r in range(PAD_R, PAD_R + rows):
            for c in range(PAD_C, PAD_C + cols, 8):
                for half in range(2):
                    span = slice(half * LANES, (half + 1) * LANES)
                    held = {}
                    for a, b in pairs:
                        for j in (a, b):
                            if j not in held:
                                held[j] = basis[j, r, c : c + 8, span]
                        term = held[a] * held[b]
                        sums[a, b] = term if (a, b) not in sums else sums[a, b] + term
        for pair in pairs:
            n = SLOT[pair]
            gram[n : n + 1, :] = jnp.sum(sums[pair], axis=0, keepdims=True)

    advance(1, 2)
    advance(2, 1)
    advance(3, 0)
    moving_2 = exchange(basis.at[3], 2, 3)
    gram[...] = jnp.zeros_like(gram)
    early = [pair for pair in PAIRS if pair[0] <= 3]
    products(early)
    for copy in moving_2:
        copy.wait_recv()
    advance(4, 2)
    advance(5, 1)
    advance(6, 0)
    products([pair for pair in PAIRS if pair[0] > 3])

    def fold(value):
        for step in (64, 32, 16, 8):
            value = value + pltpu.roll(value, step, 1)
        return value

    entry = lax.broadcasted_iota(jnp.int32, (32, LANES), 0)
    group = lax.broadcasted_iota(jnp.int32, (32, LANES), 1) // R
    chosen = group == entry % 16
    local = jnp.where(chosen, fold(gram[...]), 0.0)
    mine[0:1, :] = jnp.sum(local[0:16], axis=0, keepdims=True)
    mine[1:2, :] = jnp.sum(local[16:32], axis=0, keepdims=True)

    def gather(src, dst, index, count, send_sem, recv_sem, to):
        copies = [
            pltpu.make_async_remote_copy(
                src_ref=src,
                dst_ref=dst.at[index],
                send_sem=send_sem,
                recv_sem=recv_sem,
                device_id=to(d),
                device_id_type=pl.DeviceIdType.MESH,
            )
            for d in sorted(range(1, count), key=lambda d: -min(d, count - d))
        ]
        for copy in copies:
            copy.start()
        dst[index] = src[...]
        some = dst.at[pl.ds(0, count - 1)]
        pltpu.make_async_copy(some, some, recv_sem).wait()
        parts = [dst[n] for n in range(count)]
        while len(parts) > 1:
            parts = [parts[n] + parts[n + 1] for n in range(0, len(parts), 2)]
        return parts[0], pltpu.make_async_copy(some, some, send_sem)

    plane_sum, plane_left = gather(mine, plane_in, gy, ny, plane_send, plane_recv, lambda d: peer(0, d))
    line[...] = plane_sum
    total, line_left = gather(line, line_in, gx, nx, line_send, line_recv, lambda d: peer(d, 0))

    wide = jnp.concatenate(
        [jnp.broadcast_to(total[0:1], (16, LANES)), jnp.broadcast_to(total[1:2], (16, LANES))], axis=0
    )
    gram[...] = fold(jnp.where(chosen, wide, 0.0))
    g = lambda a, b: gram[SLOT[max(a, b), min(a, b)] : SLOT[max(a, b), min(a, b)] + 1, :]

    shift = SHIFT / SCALE

    def operate(d):
        out = []
        for j in range(len(d) + 1):
            terms = ([shift * d[j]] if j < len(d) else []) + ([d[j - 1]] if j else [])
            out.append(terms[0] if len(terms) == 1 else terms[0] + terms[1])
        return out

    def add(terms):
        while len(terms) > 1:
            terms = [terms[n] + terms[n + 1] if n + 1 < len(terms) else terms[n] for n in range(0, len(terms), 2)]
        return terms[0]

    d = [jnp.ones((1, LANES), jnp.float32)]
    y = [jnp.zeros((1, LANES), jnp.float32) for _ in range(DEGREE)]
    for _ in range(CYCLES):
        image = operate(d)
        pulled = [add([g(i, j) * d[j] for j in range(len(d))]) for i in range(len(image))]
        squares = add([d[i] * pulled[i] for i in range(len(d))])
        against = add([image[i] * pulled[i] for i in range(len(image))])
        alpha = squares / against
        half_way = [(d[i] if i < len(d) else 0.0) - alpha * image[i] for i in range(len(image))]
        turned = operate(half_way)
        pulled = [add([g(i, j) * turned[j] for j in range(len(turned))]) for i in range(len(turned))]
        along = add([half_way[i] * pulled[i] for i in range(len(half_way))])
        power = add([turned[i] * pulled[i] for i in range(len(turned))])
        omega = along / power
        for i in range(len(d)):
            y[i] = y[i] + alpha * d[i]
        for i in range(len(half_way)):
            y[i] = y[i] + omega * half_way[i]
        d = [(half_way[i] if i < len(half_way) else 0.0) - omega * turned[i] for i in range(len(turned))]

    steps = [value * inv for value in y]
    for r in range(rows):
        for c in range(0, cols, 8):
            for half in range(2):
                span = slice(half * LANES, (half + 1) * LANES)
                held = [basis[j, PAD_R + r, PAD_C + c : PAD_C + c + 8, span] for j in range(DEGREE + 1)]
                moved = add([steps[j] * held[j] for j in range(DEGREE)])
                field_out[r, c : c + 8, span] = start[PAD_R + r, PAD_C + c : PAD_C + c + 8, span] + moved
                residual_out[r, c : c + 8, span] = add([d[j] * held[j] for j in range(DEGREE + 1)])

    for copy in moving + moving_2:
        copy.wait_send()
    plane_left.wait()
    line_left.wait()


def solution(mesh):
    nx, ny = mesh.shape["gx"], mesh.shape["gy"]

    def body(adjoint_guess, velocity, leaf_rate, canopy, solid, receptors):
        rows, cols = adjoint_guess.shape[0], adjoint_guess.shape[1]
        tall, wide = rows + 2 * PAD_R, cols + 2 * PAD_C
        shape = jax.ShapeDtypeStruct(adjoint_guess.shape, jnp.float32)
        return pl.pallas_call(
            functools.partial(kernel, nx, ny, rows, cols),
            out_shape=(shape, shape),
            in_specs=[pl.BlockSpec(memory_space=pl.ANY)] * 5 + [pl.BlockSpec(memory_space=pltpu.SMEM)],
            out_specs=[pl.BlockSpec(memory_space=pltpu.VMEM)] * 2,
            scratch_shapes=[
                pltpu.VMEM((tall, wide, NZ * R), jnp.float32),
                pltpu.VMEM((DEGREE + 1, tall, wide, NZ * R), jnp.float32),
                pltpu.VMEM((tall, wide, LANES), jnp.float32),
                pltpu.VMEM((7, tall, wide, NZ * R), jnp.float32),
                pltpu.VMEM(velocity.shape, jnp.float32),
                pltpu.VMEM(leaf_rate.shape, jnp.float32),
                pltpu.VMEM(canopy.shape, jnp.int32),
                pltpu.VMEM(solid.shape, jnp.int32),
                pltpu.VMEM((32, LANES), jnp.float32),
                pltpu.VMEM((2, LANES), jnp.float32),
                pltpu.VMEM((ny, 2, LANES), jnp.float32),
                pltpu.VMEM((2, LANES), jnp.float32),
                pltpu.VMEM((nx, 2, LANES), jnp.float32),
                pltpu.SemaphoreType.DMA((5,)),
                pltpu.SemaphoreType.DMA((3, len(SIDES))),
                pltpu.SemaphoreType.DMA((3, len(SIDES))),
                pltpu.SemaphoreType.DMA,
                pltpu.SemaphoreType.DMA,
                pltpu.SemaphoreType.DMA,
                pltpu.SemaphoreType.DMA,
            ],
            compiler_params=pltpu.CompilerParams(collective_id=0, has_side_effects=True),
        )(adjoint_guess, velocity, leaf_rate, canopy, solid, receptors)

    return jax.shard_map(
        body,
        mesh=mesh,
        in_specs=(
            P("gx", "gy", None),
            P(None, "gx", "gy"),
            P("gx", "gy"),
            P("gx", "gy"),
            P("gx", "gy"),
            P(),
        ),
        out_specs=(P("gx", "gy", None), P("gx", "gy", None)),
        check_vma=False,
    )
```

time: 758 us -> 45 us (0.06)
  blocking collectives: 636 us -> 0 us
  starting transfers between devices: 68.4 us -> 0 us
  Pallas kernels: 0 us -> 42 us
  waiting for transfers between devices: 22.6 us -> 0 us
  local copies, waits for them, and re-layouts: 19.5 us -> 2.14 us
  other arithmetic: 7.63 us -> 0 us
    psum x6 -> x0, blocking collectives: 636 us -> none  [the longest x3 322 us: body(): lax.psum((per_receptor(residual, residual), per_receptor(residual, image_...]
    ppermute x28 -> x0, starting transfers between devices: 68.4 us -> none  [the longest x14 41.4 us: padded_2(): after = lax.ppermute(initial, axis, down)]
    pallas_call x0 -> x1, Pallas kernels: none -> 42 us  [body(): pl.pallas_call(functools.partial(kernel, nx, ny, rows, cols), out_shape=(...]
    ppermute x28 -> x0, waiting for transfers between devices: 22.6 us -> none  [the longest x14 19.1 us: padded_2(): after = lax.ppermute(initial, axis, down)]
    reshape x26 -> x0, local copies, waits for them, and re-layouts: 9.23 us -> none  [the longest x12 6.98 us: per_receptor(): return jnp.sum((first * second).reshape(-1, R), axis=0)]
  transfers between devices with their start and end apart: 28 -> 0, of which waited for: 11 -> 0; matrix products, arithmetic and copies ran while one was open for 1% -> 0% of each run, Pallas kernels for 0% -> 0%
where the time goes in v1:
time: 45 us; the launch traced here: 44.8 us
  Pallas kernels  42 us (93%)
  local copies, waits for them, and re-layouts  2.14 us (5%)
  between operations  0.65 us (1%)
    pallas_call x1, Pallas kernels, body(): pl.pallas_call(functools.partial(kernel, nx, ny, rows, cols), out_shape=(...  42 us
    unnamed x4, local copies, waits for them, and re-layouts  2.14 us

profile of v1, /device:TPU:1, one launch (start us, length us, event | category | flops | bytes accessed | tf_op | source)
XLA Modules:
  0.0 44.8 jit_solution(6058592820844633860)
XLA Ops:
  0.6 42.0 %shard_map.77 = (f32[4,16,256]{2,1,0:T(8,128)}, f32[4,16,256]{2,1,0:T(8,128)}) custom-call(f32[4,16,256]{2,1,0:T(8,128)} %guess.1, f32[3,4,512]{2,1,0:T(4,128)} %velocity.1, f32[4,512]{1,0:T(4,128)} %leaf.1, s32[4,512]{1,0:T(4,128)} %canopy.1, s32[4,512]{1,0:T(4,128)} %solid.1, s32[8]{0:T(128)} %receptors.1), custom_call_target="tpu_custom_call" | custom-call | tf_op jit(solution)/shard_map/pallas_call | solution.py:320
  42.6 0.0 copy-start
  42.6 1.5 %copy.10 = f32[4,16,256]{2,1,0:T(8,128)} copy(f32[4,16,256]{2,1,0:T(8,128)} %get-tuple-element.4) | data formatting | bytes 131072
  44.1 0.0 copy-done
  44.1 0.6 %copy.11 = f32[4,16,256]{2,1,0:T(8,128)} copy(f32[4,16,256]{2,1,0:T(8,128)S(1)} %copy-done) | data formatting | bytes 131072
Async XLA Ops:
  42.6 1.5 %copy-start = (f32[4,16,256]{2,1,0:T(8,128)S(1)}, f32[4,16,256]{2,1,0:T(8,128)}, u32[]{:S(2)}) copy-start(f32[4,16,256]{2,1,0:T(8,128)} %get-tuple-element.5) | copy-start | bytes 196612

commit v2 on v1

--- a/solution.py
+++ b/solution.py
@@ -19,8 +19,8 @@
 leaf_gain = 4.0
 source_gain = 32.0
 
-SHIFT = 46.5
-SCALE = 32.0
+SHIFT = 27.0
+SCALE = 16.0
 
 PAD_R = 4
 PAD_C = 8
@@ -39,13 +39,37 @@
     return pl.ds(pad, reach), pl.ds(pad + own, reach)
 
 
+def two_sum(a, b):
+    total = a + b
+    back = total - a
+    return total, (a - (total - back)) + (b - back)
+
+
+def pair_add(a, b):
+    total, error = two_sum(a[0], b[0])
+    return total, error + (a[1] + b[1])
+
+
+def split(value):
+    scaled = value * 4097.0
+    high = scaled - (scaled - value)
+    return high, value - high
+
+
+def tree(terms, join):
+    terms = list(terms)
+    while len(terms) > 1:
+        terms = [join(terms[n], terms[n + 1]) if n + 1 < len(terms) else terms[n] for n in range(0, len(terms), 2)]
+    return terms[0]
+
+
 def kernel(
     nx, ny, rows, cols,
     guess, velocity, leaf, canopy, solid, receptors,
     field_out, residual_out,
     start, basis, packed, coef, raw_vel, raw_leaf, raw_canopy, raw_solid,
-    gram, mine, plane_in, line, line_in,
-    load_sem, halo_send, halo_recv, plane_send, plane_recv, line_send, line_recv,
+    halves, gram, mine, plane_in, line, line_in,
+    load_sem, halo_send, halo_recv, plane_send, plane_recv, line_send, line_recv, met_x, met_y,
 ):
     gx = lax.axis_index("gx")
     gy = lax.axis_index("gy")
@@ -57,10 +81,28 @@
         }
 
     barrier = pltpu.get_barrier_semaphore()
-    greeted = [(0, d) for d in range(1, ny)] + [(d, 0) for d in range(1, nx)]
-    greeted += [side for side in SIDES if side[0] and side[1]]
-    for side in greeted:
+    for side in SIDES:
         pl.semaphore_signal(barrier, inc=1, device_id=peer(*side), device_id_type=pl.DeviceIdType.MESH)
+
+    def rounds(count):
+        reach, out = 1, []
+        while reach < count // 2:
+            out.append(reach)
+            reach *= 2
+        return out
+
+    def tell(n):
+        for sem, far, to in ((met_x, rounds(nx), lambda d: (d, 0)), (met_y, rounds(ny), lambda d: (0, d))):
+            if n < len(far):
+                for d in (far[n], -far[n]):
+                    pl.semaphore_signal(sem.at[n], inc=1, device_id=peer(*to(d)), device_id_type=pl.DeviceIdType.MESH)
+
+    def hear(n):
+        for sem, far in ((met_x, rounds(nx)), (met_y, rounds(ny))):
+            if n < len(far):
+                pl.semaphore_wait(sem.at[n], 2)
+
+    rest = max(len(rounds(nx)), len(rounds(ny)))
 
     own_r, own_c = pl.ds(PAD_R, rows), pl.ds(PAD_C, cols)
     loads = [
@@ -92,7 +134,7 @@
             packed[PAD_R + i, PAD_C + 8 * tile : PAD_C + 8 * tile + 8, :] = total
 
     loads[4].wait()
-    pl.semaphore_wait(barrier, len(greeted))
+    pl.semaphore_wait(barrier, len(SIDES))
 
     def exchange(ref, bank, reach):
         copies = []
@@ -114,9 +156,9 @@
             copy.start()
         return copies
 
-    moving = exchange(packed, 0, 3) + exchange(start, 1, 4)
-    for copy in moving:
-        copy.wait_recv()
+    moving_0 = exchange(packed, 0, 3)
+    moving_1 = exchange(start, 1, 4)
+    tell(0)
 
     inv = 1.0 / SCALE
     first_row = jnp.where(gx == 0, 0.0, inv)
@@ -125,9 +167,16 @@
     last_col = jnp.where(gy == ny - 1, 0.0, inv)
     tiles = (cols + 2 * PAD_C) // 8
     first_tile, last_tile = PAD_C // 8, (PAD_C + cols) // 8 - 1
-    for r in range(PAD_R - 3, PAD_R + rows + 3):
-        outer = r in (PAD_R - 3, PAD_R + rows + 2)
-        for tile in range(first_tile, last_tile + 1) if outer else range(tiles):
+    own_cells = [(r, tile) for r in range(PAD_R, PAD_R + rows) for tile in range(first_tile, last_tile + 1)]
+    all_cells = [
+        (r, tile)
+        for r in range(PAD_R - 3, PAD_R + rows + 3)
+        for tile in range(tiles)
+        if PAD_R - 3 < r < PAD_R + rows + 2 or first_tile <= tile <= last_tile
+    ]
+
+    def expand(cells):
+        for r, tile in cells:
             here = pl.ds(8 * tile, 8)
             cell = packed[r, 8 * tile : 8 * tile + 8, :]
             for half in range(2):
@@ -146,6 +195,17 @@
                 coef[4, r, here, span] = south * (jnp.where(sub == 0, first_col, inv) if tile == first_tile else inv)
                 coef[5, r, here, span] = up * (jnp.where(lane >= LANES - R, 0.0, inv) if half else inv)
                 coef[6, r, here, span] = down * (inv if half else jnp.where(lane < R, 0.0, inv))
+
+    expand(own_cells)
+    hear(0)
+    tell(1)
+    for copy in moving_0:
+        copy.wait_recv()
+    expand([cell for cell in all_cells if cell not in own_cells])
+    for copy in moving_1:
+        copy.wait_recv()
+    hear(1)
+    tell(2)
 
     def apply(ref, r, inner):
         height = cols + 2 * PAD_C
@@ -185,48 +245,77 @@
             else:
                 basis[j, r, PAD_C : PAD_C + cols, :] = apply(basis.at[j - 1], r, True)
 
-    def products(pairs):
-        sums = {}
-        for r in range(PAD_R, PAD_R + rows):
-            for c in range(PAD_C, PAD_C + cols, 8):
-                for half in range(2):
-                    span = slice(half * LANES, (half + 1) * LANES)
-                    held = {}
-                    for a, b in pairs:
-                        for j in (a, b):
-                            if j not in held:
-                                held[j] = basis[j, r, c : c + 8, span]
-                        term = held[a] * held[b]
-                        sums[a, b] = term if (a, b) not in sums else sums[a, b] + term
-        for pair in pairs:
-            n = SLOT[pair]
-            gram[n : n + 1, :] = jnp.sum(sums[pair], axis=0, keepdims=True)
-
+    def products(a):
+        spots = [
+            (r, c, half)
+            for r in range(PAD_R, PAD_R + rows)
+            for c in range(PAD_C, PAD_C + cols, 8)
+            for half in range(2)
+        ]
+        for b in range(a + 1):
+            sums[a, b] = None
+        for n, (r, c, half) in enumerate(spots):
+            high, low = split(basis[a, r, c : c + 8, half * LANES : (half + 1) * LANES])
+            halves[a, n, 0], halves[a, n, 1] = high, low
+            for b in range(a + 1):
+                if b == a:
+                    exact, cross, rest = high * high, 2.0 * (high * low), low * low
+                else:
+                    high_b, low_b = halves[b, n, 0], halves[b, n, 1]
+                    exact, cross, rest = high * high_b, high * low_b + low * high_b, low * low_b
+                if sums[a, b] is None:
+                    sums[a, b] = (exact, cross + rest)
+                else:
+                    total, error = two_sum(sums[a, b][0], exact)
+                    sums[a, b] = (total, sums[a, b][1] + (error + (cross + rest)))
+
+    def turn(value, shift, axis):
+        return pltpu.roll(value, shift % value.shape[axis], axis)
+
+    def weave(x, y, bit, axis):
+        low = ((sub if axis == 0 else lane) & bit) == 0
+        near = tuple(jnp.where(low, u, v) for u, v in zip(x, y))
+        far = tuple(jnp.where(low, turn(u, -bit, axis), turn(v, bit, axis)) for u, v in zip(x, y))
+        return pair_add(near, far)
+
+    def stack(pairs):
+        zero = jnp.zeros((8, LANES), jnp.float32)
+        got = [sums[pair] if pair else (zero, zero) for pair in pairs]
+        for bit in (4, 2, 1):
+            got = [weave(got[n], got[n + bit], bit, 0) for n in range(bit)]
+        return got[0]
+
+    sums = {}
+    blocks = [PAIRS[n : n + 8] for n in range(0, len(PAIRS), 8)]
+    blocks[-1] += [None] * (8 - len(blocks[-1]))
     advance(1, 2)
     advance(2, 1)
     advance(3, 0)
     moving_2 = exchange(basis.at[3], 2, 3)
-    gram[...] = jnp.zeros_like(gram)
-    early = [pair for pair in PAIRS if pair[0] <= 3]
-    products(early)
+    for a in range(4):
+        products(a)
+    stacked = [stack(blocks[0])]
     for copy in moving_2:
         copy.wait_recv()
+    hear(2)
+    tell(3)
     advance(4, 2)
+    products(4)
     advance(5, 1)
+    products(5)
     advance(6, 0)
-    products([pair for pair in PAIRS if pair[0] > 3])
-
-    def fold(value):
-        for step in (64, 32, 16, 8):
-            value = value + pltpu.roll(value, step, 1)
-        return value
-
-    entry = lax.broadcasted_iota(jnp.int32, (32, LANES), 0)
-    group = lax.broadcasted_iota(jnp.int32, (32, LANES), 1) // R
-    chosen = group == entry % 16
-    local = jnp.where(chosen, fold(gram[...]), 0.0)
-    mine[0:1, :] = jnp.sum(local[0:16], axis=0, keepdims=True)
-    mine[1:2, :] = jnp.sum(local[16:32], axis=0, keepdims=True)
+    products(6)
+    stacked += [stack(block) for block in blocks[1:]]
+
+    quarter = [weave(stacked[n], stacked[n + 2], 64, 1) for n in range(2)]
+    folded = weave(quarter[0], quarter[1], 32, 1)
+    folded = weave(folded, folded, 16, 1)
+    folded = weave(folded, folded, 8, 1)
+    chosen = (lane // R) % 4 == sub % 4
+    for n, value in enumerate(folded):
+        value = jnp.where(chosen, value, 0.0)
+        mine[n, 0:1, :] = jnp.sum(value[0:4], axis=0, keepdims=True)
+        mine[n, 1:2, :] = jnp.sum(value[4:8], axis=0, keepdims=True)
 
     def gather(src, dst, index, count, send_sem, recv_sem, to):
         copies = [
@@ -245,20 +334,52 @@
         dst[index] = src[...]
         some = dst.at[pl.ds(0, count - 1)]
         pltpu.make_async_copy(some, some, recv_sem).wait()
-        parts = [dst[n] for n in range(count)]
-        while len(parts) > 1:
-            parts = [parts[n] + parts[n + 1] for n in range(0, len(parts), 2)]
-        return parts[0], pltpu.make_async_copy(some, some, send_sem)
-
-    plane_sum, plane_left = gather(mine, plane_in, gy, ny, plane_send, plane_recv, lambda d: peer(0, d))
-    line[...] = plane_sum
-    total, line_left = gather(line, line_in, gx, nx, line_send, line_recv, lambda d: peer(d, 0))
-
-    wide = jnp.concatenate(
-        [jnp.broadcast_to(total[0:1], (16, LANES)), jnp.broadcast_to(total[1:2], (16, LANES))], axis=0
-    )
-    gram[...] = fold(jnp.where(chosen, wide, 0.0))
-    g = lambda a, b: gram[SLOT[max(a, b), min(a, b)] : SLOT[max(a, b), min(a, b)] + 1, :]
+        total = tree([(dst[n, 0], dst[n, 1]) for n in range(count)], pair_add)
+        return total, pltpu.make_async_copy(some, some, send_sem)
+
+    line_sum, line_left = gather(mine, line_in, gx, nx, line_send, line_recv, lambda d: peer(d, 0))
+    line[0], line[1] = line_sum
+    for n in range(3, rest):
+        hear(n)
+        tell(n + 1)
+    total, plane_left = gather(line, plane_in, gy, ny, plane_send, plane_recv, lambda d: peer(0, d))
+
+    value, error = total
+    value, error = two_sum(value, error)
+    upper = sub < 4
+    for z in range(4):
+        index = 32 * z + R * (sub % 4) + lane % R
+        spread_out = lambda x: jnp.take_along_axis(
+            jnp.where(upper, jnp.broadcast_to(x[0:1], (8, LANES)), jnp.broadcast_to(x[1:2], (8, LANES))), index, axis=1
+        )
+        here = spread_out(value)
+        gram[0, 8 * z : 8 * z + 8, :] = here
+        gram[1, 8 * z : 8 * z + 8, :] = spread_out(error)
+        gram[2, 8 * z : 8 * z + 8, :], gram[3, 8 * z : 8 * z + 8, :] = split(here)
+
+    def product(a, b):
+        whole, high, low = b
+        top = a[0] * whole
+        return top, (((a[2] * high - top) + a[2] * low + a[3] * high) + a[3] * low) + a[1] * whole
+
+    def entry(i, j):
+        n = SLOT[max(i, j), min(i, j)]
+        return tuple(gram[k, n : n + 1, :] for k in range(4))
+
+    def with_halves(values):
+        return [(value,) + split(value) for value in values]
+
+    def pull(values, count):
+        out = []
+        for i in range(count):
+            total, error = tree([product(entry(i, j), value) for j, value in enumerate(values)], pair_add)
+            total, error = two_sum(total, error)
+            out.append((total, error) + split(total))
+        return out
+
+    def inner(pulled, values):
+        total, error = tree([product(a, b) for a, b in zip(pulled, values)], pair_add)
+        return total + error
 
     shift = SHIFT / SCALE
 
@@ -269,30 +390,26 @@
             out.append(terms[0] if len(terms) == 1 else terms[0] + terms[1])
         return out
 
-    def add(terms):
-        while len(terms) > 1:
-            terms = [terms[n] + terms[n + 1] if n + 1 < len(terms) else terms[n] for n in range(0, len(terms), 2)]
-        return terms[0]
-
     d = [jnp.ones((1, LANES), jnp.float32)]
     y = [jnp.zeros((1, LANES), jnp.float32) for _ in range(DEGREE)]
     for _ in range(CYCLES):
         image = operate(d)
-        pulled = [add([g(i, j) * d[j] for j in range(len(d))]) for i in range(len(image))]
-        squares = add([d[i] * pulled[i] for i in range(len(d))])
-        against = add([image[i] * pulled[i] for i in range(len(image))])
-        alpha = squares / against
-        half_way = [(d[i] if i < len(d) else 0.0) - alpha * image[i] for i in range(len(image))]
+        held, moved = with_halves(d), with_halves(image)
+        pulled = pull(held, len(image))
+        alpha = inner(pulled, held) / inner(pulled, moved)
+        half_way = [(d[i] - alpha * image[i]) if i < len(d) else -(alpha * image[i]) for i in range(len(image))]
         turned = operate(half_way)
-        pulled = [add([g(i, j) * turned[j] for j in range(len(turned))]) for i in range(len(turned))]
-        along = add([half_way[i] * pulled[i] for i in range(len(half_way))])
-        power = add([turned[i] * pulled[i] for i in range(len(turned))])
-        omega = along / power
+        held, moved = with_halves(half_way), with_halves(turned)
+        pulled = pull(moved, len(turned))
+        omega = inner(pulled, held) / inner(pulled, moved)
         for i in range(len(d)):
             y[i] = y[i] + alpha * d[i]
         for i in range(len(half_way)):
             y[i] = y[i] + omega * half_way[i]
-        d = [(half_way[i] if i < len(half_way) else 0.0) - omega * turned[i] for i in range(len(turned))]
+        d = [
+            (half_way[i] - omega * turned[i]) if i < len(half_way) else -(omega * turned[i])
+            for i in range(len(turned))
+        ]
 
     steps = [value * inv for value in y]
     for r in range(rows):
@@ -300,11 +417,11 @@
             for half in range(2):
                 span = slice(half * LANES, (half + 1) * LANES)
                 held = [basis[j, PAD_R + r, PAD_C + c : PAD_C + c + 8, span] for j in range(DEGREE + 1)]
-                moved = add([steps[j] * held[j] for j in range(DEGREE)])
+                moved = tree([steps[j] * held[j] for j in range(DEGREE)], jnp.add)
                 field_out[r, c : c + 8, span] = start[PAD_R + r, PAD_C + c : PAD_C + c + 8, span] + moved
-                residual_out[r, c : c + 8, span] = add([d[j] * held[j] for j in range(DEGREE + 1)])
-
-    for copy in moving + moving_2:
+                residual_out[r, c : c + 8, span] = tree([d[j] * held[j] for j in range(DEGREE + 1)], jnp.add)
+
+    for copy in moving_0 + moving_1 + moving_2:
         copy.wait_send()
     plane_left.wait()
     line_left.wait()
@@ -331,11 +448,12 @@
                 pltpu.VMEM(leaf_rate.shape, jnp.float32),
                 pltpu.VMEM(canopy.shape, jnp.int32),
                 pltpu.VMEM(solid.shape, jnp.int32),
-                pltpu.VMEM((32, LANES), jnp.float32),
-                pltpu.VMEM((2, LANES), jnp.float32),
-                pltpu.VMEM((ny, 2, LANES), jnp.float32),
-                pltpu.VMEM((2, LANES), jnp.float32),
-                pltpu.VMEM((nx, 2, LANES), jnp.float32),
+                pltpu.VMEM((DEGREE + 1, rows * cols * 2 // 8, 2, 8, LANES), jnp.float32),
+                pltpu.VMEM((4, 32, LANES), jnp.float32),
+                pltpu.VMEM((2, 2, LANES), jnp.float32),
+                pltpu.VMEM((ny, 2, 2, LANES), jnp.float32),
+                pltpu.VMEM((2, 2, LANES), jnp.float32),
+                pltpu.VMEM((nx, 2, 2, LANES), jnp.float32),
                 pltpu.SemaphoreType.DMA((5,)),
                 pltpu.SemaphoreType.DMA((3, len(SIDES))),
                 pltpu.SemaphoreType.DMA((3, len(SIDES))),
@@ -343,6 +461,8 @@
                 pltpu.SemaphoreType.DMA,
                 pltpu.SemaphoreType.DMA,
                 pltpu.SemaphoreType.DMA,
+                pltpu.SemaphoreType.REGULAR((8,)),
+                pltpu.SemaphoreType.REGULAR((8,)),
             ],
             compiler_params=pltpu.CompilerParams(collective_id=0, has_side_effects=True),
         )(adjoint_guess, velocity, leaf_rate, canopy, solid, receptors)

time: 45 us -> 43.6 us (0.969)
  Pallas kernels: 42 us -> 40.6 us
    pallas_call x1, Pallas kernels: 42 us -> 40.6 us  [body(): pl.pallas_call(functools.partial(kernel, nx, ny, rows, cols), out_shape=(...]
where the time goes in v2:
time: 43.6 us; the launch traced here: 43.4 us
  Pallas kernels  40.6 us (93%)
  local copies, waits for them, and re-layouts  2.14 us (5%)
  between operations  0.65 us (1%)
    pallas_call x1, Pallas kernels, body(): pl.pallas_call(functools.partial(kernel, nx, ny, rows, cols), out_shape=(...  40.6 us
    unnamed x4, local copies, waits for them, and re-layouts  2.14 us

profile of v2, /device:TPU:1, one launch (start us, length us, event | category | flops | bytes accessed | tf_op | source)
XLA Modules:
  0.0 43.4 jit_solution(6959325842093028418)
XLA Ops:
  0.6 40.6 %shard_map.77 = (f32[4,16,256]{2,1,0:T(8,128)}, f32[4,16,256]{2,1,0:T(8,128)}) custom-call(f32[4,16,256]{2,1,0:T(8,128)} %guess.1, f32[3,4,512]{2,1,0:T(4,128)} %velocity.1, f32[4,512]{1,0:T(4,128)} %leaf.1, s32[4,512]{1,0:T(4,128)} %canopy.1, s32[4,512]{1,0:T(4,128)} %solid.1, s32[8]{0:T(128)} %receptors.1), custom_call_target="tpu_custom_call" | custom-call | tf_op jit(solution)/shard_map/pallas_call | solution.py:437
  41.2 0.0 copy-start
  41.3 1.5 %copy.10 = f32[4,16,256]{2,1,0:T(8,128)} copy(f32[4,16,256]{2,1,0:T(8,128)} %get-tuple-element.4) | data formatting | bytes 131072
  42.8 0.0 copy-done
  42.8 0.6 %copy.11 = f32[4,16,256]{2,1,0:T(8,128)} copy(f32[4,16,256]{2,1,0:T(8,128)S(1)} %copy-done) | data formatting | bytes 131072
Async XLA Ops:
  41.2 1.5 %copy-start = (f32[4,16,256]{2,1,0:T(8,128)S(1)}, f32[4,16,256]{2,1,0:T(8,128)}, u32[]{:S(2)}) copy-start(f32[4,16,256]{2,1,0:T(8,128)} %get-tuple-element.5) | copy-start | bytes 196612

commit v3 on v2

--- a/solution.py
+++ b/solution.py
@@ -28,7 +28,7 @@
 
 PAIRS = [(a, b) for a in range(DEGREE + 1) for b in range(a + 1)]
 SLOT = {pair: n for n, pair in enumerate(PAIRS)}
-SIDES = [(dx, dy) for dx in (1, -1, 0) for dy in (0, 1, -1) if (dx, dy) != (0, 0)]
+SIDES = [(1, 1), (1, -1), (-1, 1), (-1, -1), (0, 1), (0, -1), (1, 0), (-1, 0)]
 
 
 def window(delta, reach, own, pad):
@@ -68,7 +68,7 @@
     guess, velocity, leaf, canopy, solid, receptors,
     field_out, residual_out,
     start, basis, packed, coef, raw_vel, raw_leaf, raw_canopy, raw_solid,
-    halves, gram, mine, plane_in, line, line_in,
+    halves, gram, mine, plane_in, line, line_in, aims,
     load_sem, halo_send, halo_recv, plane_send, plane_recv, line_send, line_recv, met_x, met_y,
 ):
     gx = lax.axis_index("gx")
@@ -80,29 +80,52 @@
             "gy": lax.rem(gy + dy + ny, ny) if dy else gy,
         }
 
+    def inside(dy):
+        return jnp.logical_and(gy + dy >= 0, gy + dy < ny)
+
+    def where_inside(dy, act):
+        if dy:
+            pl.when(inside(dy))(act)
+        else:
+            act()
+
+    def signal(sem, side):
+        where_inside(
+            side[1],
+            lambda: pl.semaphore_signal(sem, inc=1, device_id=peer(*side), device_id_type=pl.DeviceIdType.MESH),
+        )
+
+    def both(d):
+        return inside(d).astype(jnp.int32) + inside(-d).astype(jnp.int32)
+
     barrier = pltpu.get_barrier_semaphore()
     for side in SIDES:
-        pl.semaphore_signal(barrier, inc=1, device_id=peer(*side), device_id_type=pl.DeviceIdType.MESH)
-
-    def rounds(count):
+        signal(barrier, side)
+
+    def rounds(most):
         reach, out = 1, []
-        while reach < count // 2:
+        while reach < most:
             out.append(reach)
             reach *= 2
         return out
 
+    rounds_x, rounds_y = rounds(nx // 2), rounds(ny - 1)
+
     def tell(n):
-        for sem, far, to in ((met_x, rounds(nx), lambda d: (d, 0)), (met_y, rounds(ny), lambda d: (0, d))):
-            if n < len(far):
-                for d in (far[n], -far[n]):
-                    pl.semaphore_signal(sem.at[n], inc=1, device_id=peer(*to(d)), device_id_type=pl.DeviceIdType.MESH)
+        if n < len(rounds_x):
+            for d in (rounds_x[n], -rounds_x[n]):
+                signal(met_x.at[n], (d, 0))
+        if n < len(rounds_y):
+            for d in (rounds_y[n], -rounds_y[n]):
+                signal(met_y.at[n], (0, d))
 
     def hear(n):
-        for sem, far in ((met_x, rounds(nx)), (met_y, rounds(ny))):
-            if n < len(far):
-                pl.semaphore_wait(sem.at[n], 2)
-
-    rest = max(len(rounds(nx)), len(rounds(ny)))
+        if n < len(rounds_x):
+            pl.semaphore_wait(met_x.at[n], 2)
+        if n < len(rounds_y):
+            pl.semaphore_wait(met_y.at[n], both(rounds_y[n]))
+
+    rest = max(len(rounds_x), len(rounds_y))
 
     own_r, own_c = pl.ds(PAD_R, rows), pl.ds(PAD_C, cols)
     loads = [
@@ -111,9 +134,17 @@
         pltpu.make_async_copy(canopy, raw_canopy, load_sem.at[2]),
         pltpu.make_async_copy(solid, raw_solid, load_sem.at[3]),
         pltpu.make_async_copy(guess, start.at[own_r, own_c], load_sem.at[4]),
+        pltpu.make_async_copy(receptors, aims, load_sem.at[5]),
     ]
     for copy in loads:
         copy.start()
+
+    def clear(side):
+        for ref in (start, packed, basis.at[3]):
+            ref[:, side, :] = jnp.zeros((ref.shape[0], PAD_C, ref.shape[2]), jnp.float32)
+
+    pl.when(gy == 0)(lambda: clear(slice(0, PAD_C)))
+    pl.when(gy == ny - 1)(lambda: clear(slice(PAD_C + cols, 2 * PAD_C + cols)))
 
     sub = lax.broadcasted_iota(jnp.int32, (8, LANES), 0)
     lane = lax.broadcasted_iota(jnp.int32, (8, LANES), 1)
@@ -133,8 +164,9 @@
                 total = value if total is None else jnp.where(lane // NZ == n, value, total)
             packed[PAD_R + i, PAD_C + 8 * tile : PAD_C + 8 * tile + 8, :] = total
 
-    loads[4].wait()
-    pl.semaphore_wait(barrier, len(SIDES))
+    for copy in loads[4:]:
+        copy.wait()
+    pl.semaphore_wait(barrier, 3 * (1 + both(1)) - 1)
 
     def exchange(ref, bank, reach):
         copies = []
@@ -143,18 +175,25 @@
             src_r, dst_r = window(dx, near, rows, PAD_R)
             src_c, dst_c = window(dy, near, cols, PAD_C)
             copies.append(
-                pltpu.make_async_remote_copy(
-                    src_ref=ref.at[src_r, src_c],
-                    dst_ref=ref.at[dst_r, dst_c],
-                    send_sem=halo_send.at[bank, n],
-                    recv_sem=halo_recv.at[bank, n],
-                    device_id=peer(dx, dy),
-                    device_id_type=pl.DeviceIdType.MESH,
+                (
+                    dy,
+                    pltpu.make_async_remote_copy(
+                        src_ref=ref.at[src_r, src_c],
+                        dst_ref=ref.at[dst_r, dst_c],
+                        send_sem=halo_send.at[bank, n],
+                        recv_sem=halo_recv.at[bank, n],
+                        device_id=peer(dx, dy),
+                        device_id_type=pl.DeviceIdType.MESH,
+                    ),
                 )
             )
-        for copy in copies:
-            copy.start()
+        for dy, copy in copies:
+            where_inside(dy, copy.start)
         return copies
+
+    def arrive(copies):
+        for dy, copy in copies:
+            where_inside(-dy, copy.wait_recv)
 
     moving_0 = exchange(packed, 0, 3)
     moving_1 = exchange(start, 1, 4)
@@ -199,11 +238,9 @@
     expand(own_cells)
     hear(0)
     tell(1)
-    for copy in moving_0:
-        copy.wait_recv()
+    arrive(moving_0)
     expand([cell for cell in all_cells if cell not in own_cells])
-    for copy in moving_1:
-        copy.wait_recv()
+    arrive(moving_1)
     hear(1)
     tell(2)
 
@@ -232,7 +269,7 @@
     place = lax.broadcasted_iota(jnp.int32, (height, NZ * R), 0) + (gy * cols - PAD_C)
     aim = jnp.full((height, NZ * R), -1 << 30, jnp.int32)
     for q in range(R):
-        aim = jnp.where(lanes == R + q, receptors[q], aim)
+        aim = jnp.where(lanes == R + q, aims[q], aim)
     aim = aim - place
     for r in range(PAD_R - 3, PAD_R + rows + 3):
         source = jnp.where(aim == (gx * rows + (r - PAD_R)) * (ny * cols), source_gain, 0.0)
@@ -295,8 +332,7 @@
     for a in range(4):
         products(a)
     stacked = [stack(blocks[0])]
-    for copy in moving_2:
-        copy.wait_recv()
+    arrive(moving_2)
     hear(2)
     tell(3)
     advance(4, 2)
@@ -305,6 +341,8 @@
     products(5)
     advance(6, 0)
     products(6)
+    hear(3)
+    tell(4)
     stacked += [stack(block) for block in blocks[1:]]
 
     quarter = [weave(stacked[n], stacked[n + 2], 64, 1) for n in range(2)]
@@ -339,7 +377,7 @@
 
     line_sum, line_left = gather(mine, line_in, gx, nx, line_send, line_recv, lambda d: peer(d, 0))
     line[0], line[1] = line_sum
-    for n in range(3, rest):
+    for n in range(4, rest):
         hear(n)
         tell(n + 1)
     total, plane_left = gather(line, plane_in, gy, ny, plane_send, plane_recv, lambda d: peer(0, d))
@@ -421,8 +459,8 @@
                 field_out[r, c : c + 8, span] = start[PAD_R + r, PAD_C + c : PAD_C + c + 8, span] + moved
                 residual_out[r, c : c + 8, span] = tree([d[j] * held[j] for j in range(DEGREE + 1)], jnp.add)
 
-    for copy in moving_0 + moving_1 + moving_2:
-        copy.wait_send()
+    for dy, copy in moving_0 + moving_1 + moving_2:
+        where_inside(dy, copy.wait_send)
     plane_left.wait()
     line_left.wait()
 
@@ -430,14 +468,15 @@
 def solution(mesh):
     nx, ny = mesh.shape["gx"], mesh.shape["gy"]
 
-    def body(adjoint_guess, velocity, leaf_rate, canopy, solid, receptors):
+    def body(*arrays):
+        adjoint_guess, velocity, leaf_rate, canopy, solid, receptors = arrays
         rows, cols = adjoint_guess.shape[0], adjoint_guess.shape[1]
         tall, wide = rows + 2 * PAD_R, cols + 2 * PAD_C
         shape = jax.ShapeDtypeStruct(adjoint_guess.shape, jnp.float32)
         return pl.pallas_call(
             functools.partial(kernel, nx, ny, rows, cols),
             out_shape=(shape, shape),
-            in_specs=[pl.BlockSpec(memory_space=pl.ANY)] * 5 + [pl.BlockSpec(memory_space=pltpu.SMEM)],
+            in_specs=[pl.BlockSpec(memory_space=pltpu.HBM)] * 6,
             out_specs=[pl.BlockSpec(memory_space=pltpu.VMEM)] * 2,
             scratch_shapes=[
                 pltpu.VMEM((tall, wide, NZ * R), jnp.float32),
@@ -454,7 +493,8 @@
                 pltpu.VMEM((ny, 2, 2, LANES), jnp.float32),
                 pltpu.VMEM((2, 2, LANES), jnp.float32),
                 pltpu.VMEM((nx, 2, 2, LANES), jnp.float32),
-                pltpu.SemaphoreType.DMA((5,)),
+                pltpu.SMEM(receptors.shape, jnp.int32),
+                pltpu.SemaphoreType.DMA((6,)),
                 pltpu.SemaphoreType.DMA((3, len(SIDES))),
                 pltpu.SemaphoreType.DMA((3, len(SIDES))),
                 pltpu.SemaphoreType.DMA,
@@ -464,8 +504,8 @@
                 pltpu.SemaphoreType.REGULAR((8,)),
                 pltpu.SemaphoreType.REGULAR((8,)),
             ],
-            compiler_params=pltpu.CompilerParams(collective_id=0, has_side_effects=True),
-        )(adjoint_guess, velocity, leaf_rate, canopy, solid, receptors)
+            compiler_params=pltpu.CompilerParams(collective_id=0, has_side_effects=True, vmem_limit_bytes=16 << 20),
+        )(*(pltpu.with_memory_space_constraint(array, pltpu.HBM) for array in arrays))
 
     return jax.shard_map(
         body,

time: 43.6 us -> 40.7 us (0.933)
  Pallas kernels: 40.6 us -> 38.6 us
  local copies, waits for them, and re-layouts: 2.14 us -> 1.26 us
    pallas_call x1, Pallas kernels: 40.6 us -> 38.6 us  [body(): pl.pallas_call(functools.partial(kernel, nx, ny, rows, cols), out_shape=(...]
    unnamed x4 -> x2, local copies, waits for them, and re-layouts: 2.14 us -> 1.26 us
where the time goes in v3:
time: 40.7 us; the launch traced here: 40.5 us
  Pallas kernels  38.6 us (95%)
  local copies, waits for them, and re-layouts  1.26 us (3%)
  between operations  0.64 us (2%)
    pallas_call x1, Pallas kernels, body(): pl.pallas_call(functools.partial(kernel, nx, ny, rows, cols), out_shape=(...  38.6 us
    unnamed x2, local copies, waits for them, and re-layouts  1.26 us

profile of v3, /device:TPU:1, one launch (start us, length us, event | category | flops | bytes accessed | tf_op | source)
XLA Modules:
  0.0 40.5 jit_solution(7863759900149966914)
XLA Ops:
  0.6 38.6 %shard_map.77 = (f32[4,16,256]{2,1,0:T(8,128)S(1)}, f32[4,16,256]{2,1,0:T(8,128)S(1)}) custom-call(f32[4,16,256]{2,1,0:T(8,128)} %guess.1, f32[3,4,512]{2,1,0:T(4,128)} %velocity.1, f32[4,512]{1,0:T(4,128)} %leaf.1, s32[4,512]{1,0:T(4,128)} %canopy.1, s32[4,512]{1,0:T(4,128)} %solid.1, s32[8]{0:T(128)} %receptors.1), custom_call_target="tpu_custom_call" | custom-call | tf_op jit(solution)/shard_map/pallas_call | solution.py:476
  39.3 0.6 %copy.10 = f32[4,16,256]{2,1,0:T(8,128)} copy(f32[4,16,256]{2,1,0:T(8,128)S(1)} %get-tuple-element.4) | data formatting | bytes 131072
  39.9 0.6 %copy.11 = f32[4,16,256]{2,1,0:T(8,128)} copy(f32[4,16,256]{2,1,0:T(8,128)S(1)} %get-tuple-element.5) | data formatting | bytes 131072

commit v4 on v3

--- a/solution.py
+++ b/solution.py
@@ -22,6 +22,7 @@
 SHIFT = 27.0
 SCALE = 16.0
 
+FIRST = 4
 PAD_R = 4
 PAD_C = 8
 LANES = 128
@@ -66,7 +67,7 @@
 def kernel(
     nx, ny, rows, cols,
     guess, velocity, leaf, canopy, solid, receptors,
-    field_out, residual_out,
+    out,
     start, basis, packed, coef, raw_vel, raw_leaf, raw_canopy, raw_solid,
     halves, gram, mine, plane_in, line, line_in, aims,
     load_sem, halo_send, halo_recv, plane_send, plane_recv, line_send, line_recv, met_x, met_y,
@@ -111,21 +112,26 @@
 
     rounds_x, rounds_y = rounds(nx // 2), rounds(ny - 1)
 
-    def tell(n):
+    def tell_x(n):
         if n < len(rounds_x):
             for d in (rounds_x[n], -rounds_x[n]):
                 signal(met_x.at[n], (d, 0))
+
+    def tell_y(n):
         if n < len(rounds_y):
             for d in (rounds_y[n], -rounds_y[n]):
                 signal(met_y.at[n], (0, d))
 
-    def hear(n):
+    def pass_x(n):
         if n < len(rounds_x):
             pl.semaphore_wait(met_x.at[n], 2)
+            tell_x(n + 1)
+
+    def pass_y(n):
         if n < len(rounds_y):
             pl.semaphore_wait(met_y.at[n], both(rounds_y[n]))
-
-    rest = max(len(rounds_x), len(rounds_y))
+            tell_y(n + 1)
+
 
     own_r, own_c = pl.ds(PAD_R, rows), pl.ds(PAD_C, cols)
     loads = [
@@ -140,7 +146,7 @@
         copy.start()
 
     def clear(side):
-        for ref in (start, packed, basis.at[3]):
+        for ref in (start, packed, basis.at[FIRST - 1]):
             ref[:, side, :] = jnp.zeros((ref.shape[0], PAD_C, ref.shape[2]), jnp.float32)
 
     pl.when(gy == 0)(lambda: clear(slice(0, PAD_C)))
@@ -167,6 +173,8 @@
     for copy in loads[4:]:
         copy.wait()
     pl.semaphore_wait(barrier, 3 * (1 + both(1)) - 1)
+
+    reach = max(FIRST - 1, DEGREE - FIRST)
 
     def exchange(ref, bank, reach):
         copies = []
@@ -195,9 +203,10 @@
         for dy, copy in copies:
             where_inside(-dy, copy.wait_recv)
 
-    moving_0 = exchange(packed, 0, 3)
-    moving_1 = exchange(start, 1, 4)
-    tell(0)
+    moving_0 = exchange(packed, 0, reach)
+    moving_1 = exchange(start, 1, FIRST)
+    tell_x(0)
+    tell_y(0)
 
     inv = 1.0 / SCALE
     first_row = jnp.where(gx == 0, 0.0, inv)
@@ -209,9 +218,9 @@
     own_cells = [(r, tile) for r in range(PAD_R, PAD_R + rows) for tile in range(first_tile, last_tile + 1)]
     all_cells = [
         (r, tile)
-        for r in range(PAD_R - 3, PAD_R + rows + 3)
+        for r in range(PAD_R - reach, PAD_R + rows + reach)
         for tile in range(tiles)
-        if PAD_R - 3 < r < PAD_R + rows + 2 or first_tile <= tile <= last_tile
+        if PAD_R - reach < r < PAD_R + rows + reach - 1 or first_tile <= tile <= last_tile
     ]
 
     def expand(cells):
@@ -236,13 +245,13 @@
                 coef[6, r, here, span] = down * (inv if half else jnp.where(lane < R, 0.0, inv))
 
     expand(own_cells)
-    hear(0)
-    tell(1)
+    pass_x(0)
+    pass_y(0)
     arrive(moving_0)
     expand([cell for cell in all_cells if cell not in own_cells])
+    pass_y(1)
     arrive(moving_1)
-    hear(1)
-    tell(2)
+    pass_x(1)
 
     def apply(ref, r, inner):
         height = cols + 2 * PAD_C
@@ -271,7 +280,7 @@
     for q in range(R):
         aim = jnp.where(lanes == R + q, aims[q], aim)
     aim = aim - place
-    for r in range(PAD_R - 3, PAD_R + rows + 3):
+    for r in range(PAD_R - FIRST + 1, PAD_R + rows + FIRST - 1):
         source = jnp.where(aim == (gx * rows + (r - PAD_R)) * (ny * cols), source_gain, 0.0)
         basis[0, r] = source - (SCALE * apply(start, r, False) + SHIFT * start[r])
 
@@ -325,25 +334,20 @@
     sums = {}
     blocks = [PAIRS[n : n + 8] for n in range(0, len(PAIRS), 8)]
     blocks[-1] += [None] * (8 - len(blocks[-1]))
-    advance(1, 2)
-    advance(2, 1)
-    advance(3, 0)
-    moving_2 = exchange(basis.at[3], 2, 3)
-    for a in range(4):
+    for j in range(1, FIRST):
+        advance(j, FIRST - 1 - j)
+    moving_2 = exchange(basis.at[FIRST - 1], 2, DEGREE + 1 - FIRST)
+    for a in range(FIRST):
         products(a)
-    stacked = [stack(blocks[0])]
+    stacked = [stack(block) for block in blocks if block[-1] and block[-1][0] < FIRST]
+    pass_y(2)
     arrive(moving_2)
-    hear(2)
-    tell(3)
-    advance(4, 2)
-    products(4)
-    advance(5, 1)
-    products(5)
-    advance(6, 0)
-    products(6)
-    hear(3)
-    tell(4)
-    stacked += [stack(block) for block in blocks[1:]]
+    pass_x(2)
+    pass_y(3)
+    for j in range(FIRST, DEGREE + 1):
+        advance(j, DEGREE - j)
+        products(j)
+    stacked += [stack(block) for block in blocks[len(stacked) :]]
 
     quarter = [weave(stacked[n], stacked[n + 2], 64, 1) for n in range(2)]
     folded = weave(quarter[0], quarter[1], 32, 1)
@@ -375,11 +379,12 @@
         total = tree([(dst[n, 0], dst[n, 1]) for n in range(count)], pair_add)
         return total, pltpu.make_async_copy(some, some, send_sem)
 
+    for n in range(3, len(rounds_x)):
+        pass_x(n)
     line_sum, line_left = gather(mine, line_in, gx, nx, line_send, line_recv, lambda d: peer(d, 0))
     line[0], line[1] = line_sum
-    for n in range(4, rest):
-        hear(n)
-        tell(n + 1)
+    for n in range(4, len(rounds_y)):
+        pass_y(n)
     total, plane_left = gather(line, plane_in, gy, ny, plane_send, plane_recv, lambda d: peer(0, d))
 
     value, error = total
@@ -456,8 +461,8 @@
                 span = slice(half * LANES, (half + 1) * LANES)
                 held = [basis[j, PAD_R + r, PAD_C + c : PAD_C + c + 8, span] for j in range(DEGREE + 1)]
                 moved = tree([steps[j] * held[j] for j in range(DEGREE)], jnp.add)
-                field_out[r, c : c + 8, span] = start[PAD_R + r, PAD_C + c : PAD_C + c + 8, span] + moved
-                residual_out[r, c : c + 8, span] = tree([d[j] * held[j] for j in range(DEGREE + 1)], jnp.add)
+                out[0, r, c : c + 8, span] = start[PAD_R + r, PAD_C + c : PAD_C + c + 8, span] + moved
+                out[1, r, c : c + 8, span] = tree([d[j] * held[j] for j in range(DEGREE + 1)], jnp.add)
 
     for dy, copy in moving_0 + moving_1 + moving_2:
         where_inside(dy, copy.wait_send)
@@ -472,12 +477,12 @@
         adjoint_guess, velocity, leaf_rate, canopy, solid, receptors = arrays
         rows, cols = adjoint_guess.shape[0], adjoint_guess.shape[1]
         tall, wide = rows + 2 * PAD_R, cols + 2 * PAD_C
-        shape = jax.ShapeDtypeStruct(adjoint_guess.shape, jnp.float32)
-        return pl.pallas_call(
+        shape = jax.ShapeDtypeStruct((2,) + adjoint_guess.shape, jnp.float32)
+        both = pl.pallas_call(
             functools.partial(kernel, nx, ny, rows, cols),
-            out_shape=(shape, shape),
+            out_shape=shape,
             in_specs=[pl.BlockSpec(memory_space=pltpu.HBM)] * 6,
-            out_specs=[pl.BlockSpec(memory_space=pltpu.VMEM)] * 2,
+            out_specs=pl.BlockSpec(memory_space=pltpu.VMEM),
             scratch_shapes=[
                 pltpu.VMEM((tall, wide, NZ * R), jnp.float32),
                 pltpu.VMEM((DEGREE + 1, tall, wide, NZ * R), jnp.float32),
@@ -506,6 +511,7 @@
             ],
             compiler_params=pltpu.CompilerParams(collective_id=0, has_side_effects=True, vmem_limit_bytes=16 << 20),
         )(*(pltpu.with_memory_space_constraint(array, pltpu.HBM) for array in arrays))
+        return both[0], both[1]
 
     return jax.shard_map(
         body,

time: 40.7 us -> 39.8 us (0.978)
  local copies, waits for them, and re-layouts: 1.26 us -> 0.66 us
    unnamed x2 -> x0, local copies, waits for them, and re-layouts: 1.26 us -> none
    squeeze x0 -> x1, local copies, waits for them, and re-layouts: none -> 0.66 us  [body(): return (both[0], both[1])]
where the time goes in v4:
time: 39.8 us; the launch traced here: 39.6 us
  Pallas kernels  38.3 us (96%)
  local copies, waits for them, and re-layouts  0.66 us (2%)
  between operations  0.64 us (2%)
    pallas_call x1, Pallas kernels, body(): pl.pallas_call(functools.partial(kernel, nx, ny, rows, cols), out_shape=s...  38.3 us

profile of v4, /device:TPU:1, one launch (start us, length us, event | category | flops | bytes accessed | tf_op | source)
XLA Modules:
  0.0 39.6 jit_solution(17877349211112992492)
XLA Ops:
  0.6 38.3 %shard_map.77 = f32[2,4,16,256]{3,2,1,0:T(8,128)S(1)} custom-call(f32[4,16,256]{2,1,0:T(8,128)} %guess.1, f32[3,4,512]{2,1,0:T(4,128)} %velocity.1, f32[4,512]{1,0:T(4,128)} %leaf.1, s32[4,512]{1,0:T(4,128)} %canopy.1, s32[4,512]{1,0:T(4,128)} %solid.1, s32[8]{0:T(128)} %receptors.1), custom_call_target="tpu_custom_call" | custom-call | tf_op jit(solution)/shard_map/pallas_call | solution.py:481
  39.0 0.7 %slice_bitcast_fusion = (f32[4,16,256]{2,1,0:T(8,128)}, f32[4,16,256]{2,1,0:T(8,128)}) fusion(f32[2,4,16,256]{3,2,1,0:T(8,128)S(1)} %shard_map.77), kind=kLoop, calls=%fused_computation | loop fusion | bytes 262144 | tf_op jit(solution)/shard_map/squeeze | solution.py:514

commit v5 on v4

--- a/solution.py
+++ b/solution.py
@@ -253,10 +253,9 @@
     arrive(moving_1)
     pass_x(1)
 
-    def apply(ref, r, inner):
+    def apply(ref, r, cut):
         height = cols + 2 * PAD_C
         width = NZ * R
-        cut = slice(PAD_C, PAD_C + cols) if inner else slice(0, height)
         centre = ref[r]
         north = pltpu.roll(centre, height - 1, 0)[cut]
         south = pltpu.roll(centre, 1, 0)[cut]
@@ -282,14 +281,14 @@
     aim = aim - place
     for r in range(PAD_R - FIRST + 1, PAD_R + rows + FIRST - 1):
         source = jnp.where(aim == (gx * rows + (r - PAD_R)) * (ny * cols), source_gain, 0.0)
-        basis[0, r] = source - (SCALE * apply(start, r, False) + SHIFT * start[r])
+        cut = slice(PAD_C, PAD_C + cols) if r in (PAD_R - FIRST + 1, PAD_R + rows + FIRST - 2) else slice(0, height)
+        basis[0, r, cut, :] = source[cut] - (SCALE * apply(start, r, cut) + SHIFT * start[r, cut, :])
 
     def advance(j, reach):
         for r in range(PAD_R - reach, PAD_R + rows + reach):
-            if reach:
-                basis[j, r] = apply(basis.at[j - 1], r, False)
-            else:
-                basis[j, r, PAD_C : PAD_C + cols, :] = apply(basis.at[j - 1], r, True)
+            outer = reach == 0 or r in (PAD_R - reach, PAD_R + rows + reach - 1)
+            cut = slice(PAD_C, PAD_C + cols) if outer else slice(0, height)
+            basis[j, r, cut, :] = apply(basis.at[j - 1], r, cut)
 
     def products(a):
         spots = [
@@ -298,22 +297,22 @@
             for c in range(PAD_C, PAD_C + cols, 8)
             for half in range(2)
         ]
-        for b in range(a + 1):
-            sums[a, b] = None
-        for n, (r, c, half) in enumerate(spots):
-            high, low = split(basis[a, r, c : c + 8, half * LANES : (half + 1) * LANES])
+        values = [basis[a, r, c : c + 8, half * LANES : (half + 1) * LANES] for r, c, half in spots]
+        peaks[a] = tree([jnp.abs(value) for value in values], jnp.maximum)
+        anchors = [(4.0 * len(spots)) * (peaks[a] * peaks[b]) for b in range(a + 1)]
+        totals, errors = list(anchors), [None] * (a + 1)
+        for n, value in enumerate(values):
+            high, low = split(value)
             halves[a, n, 0], halves[a, n, 1] = high, low
             for b in range(a + 1):
-                if b == a:
-                    exact, cross, rest = high * high, 2.0 * (high * low), low * low
-                else:
-                    high_b, low_b = halves[b, n, 0], halves[b, n, 1]
-                    exact, cross, rest = high * high_b, high * low_b + low * high_b, low * low_b
-                if sums[a, b] is None:
-                    sums[a, b] = (exact, cross + rest)
-                else:
-                    total, error = two_sum(sums[a, b][0], exact)
-                    sums[a, b] = (total, sums[a, b][1] + (error + (cross + rest)))
+                high_b, low_b = (high, low) if b == a else (halves[b, n, 0], halves[b, n, 1])
+                exact = high * high_b
+                small = high * low_b + low * (high_b + low_b)
+                total = totals[b] + exact
+                small = small + (exact - (total - totals[b]))
+                totals[b], errors[b] = total, small if n == 0 else errors[b] + small
+        for b in range(a + 1):
+            sums[a, b] = (totals[b] - anchors[b], errors[b])
 
     def turn(value, shift, axis):
         return pltpu.roll(value, shift % value.shape[axis], axis)
@@ -331,7 +330,7 @@
             got = [weave(got[n], got[n + bit], bit, 0) for n in range(bit)]
         return got[0]
 
-    sums = {}
+    sums, peaks = {}, {}
     blocks = [PAIRS[n : n + 8] for n in range(0, len(PAIRS), 8)]
     blocks[-1] += [None] * (8 - len(blocks[-1]))
     for j in range(1, FIRST):

time: 39.8 us -> 39.6 us (level)
  no operation moved by 1% of the time
where the time goes in v5:
time: 39.6 us; the launch traced here: 39.4 us
  Pallas kernels  38.1 us (96%)
  local copies, waits for them, and re-layouts  0.66 us (2%)
  between operations  0.64 us (2%)
    pallas_call x1, Pallas kernels, body(): pl.pallas_call(functools.partial(kernel, nx, ny, rows, cols), out_shape=s...  38.1 us

profile of v5, /device:TPU:1, one launch (start us, length us, event | category | flops | bytes accessed | tf_op | source)
XLA Modules:
  0.0 39.4 jit_solution(7217247406369632047)
XLA Ops:
  0.6 38.1 %shard_map.77 = f32[2,4,16,256]{3,2,1,0:T(8,128)S(1)} custom-call(f32[4,16,256]{2,1,0:T(8,128)} %guess.1, f32[3,4,512]{2,1,0:T(4,128)} %velocity.1, f32[4,512]{1,0:T(4,128)} %leaf.1, s32[4,512]{1,0:T(4,128)} %canopy.1, s32[4,512]{1,0:T(4,128)} %solid.1, s32[8]{0:T(128)} %receptors.1), custom_call_target="tpu_custom_call" | custom-call | tf_op jit(solution)/shard_map/pallas_call | solution.py:480
  38.8 0.7 %slice_bitcast_fusion = (f32[4,16,256]{2,1,0:T(8,128)}, f32[4,16,256]{2,1,0:T(8,128)}) fusion(f32[2,4,16,256]{3,2,1,0:T(8,128)S(1)} %shard_map.77), kind=kLoop, calls=%fused_computation | loop fusion | bytes 262144 | tf_op jit(solution)/shard_map/squeeze | solution.py:513

commit v6 on v5

--- a/solution.py
+++ b/solution.py
@@ -195,16 +195,24 @@
                     ),
                 )
             )
+        return copies
+
+    def depart(copies):
         for dy, copy in copies:
             where_inside(dy, copy.start)
-        return copies
 
     def arrive(copies):
         for dy, copy in copies:
             where_inside(-dy, copy.wait_recv)
 
+    straight = [n for n, (dx, dy) in enumerate(SIDES) if not dy]
+    slanted = [n for n, (dx, dy) in enumerate(SIDES) if dy]
+
     moving_0 = exchange(packed, 0, reach)
     moving_1 = exchange(start, 1, FIRST)
+    for group in (slanted, straight):
+        depart([moving_0[n] for n in group])
+        depart([moving_1[n] for n in group])
     tell_x(0)
     tell_y(0)
 
@@ -247,8 +255,11 @@
     expand(own_cells)
     pass_x(0)
     pass_y(0)
-    arrive(moving_0)
-    expand([cell for cell in all_cells if cell not in own_cells])
+    arrive([moving_0[n] for n in straight])
+    middle_cells = [cell for cell in all_cells if cell not in own_cells and first_tile <= cell[1] <= last_tile]
+    expand(middle_cells)
+    arrive([moving_0[n] for n in slanted])
+    expand([cell for cell in all_cells if cell not in own_cells + middle_cells])
     pass_y(1)
     arrive(moving_1)
     pass_x(1)
@@ -336,6 +347,7 @@
     for j in range(1, FIRST):
         advance(j, FIRST - 1 - j)
     moving_2 = exchange(basis.at[FIRST - 1], 2, DEGREE + 1 - FIRST)
+    depart(moving_2)
     for a in range(FIRST):
         products(a)
     stacked = [stack(block) for block in blocks if block[-1] and block[-1][0] < FIRST]

time: 39.6 us -> 39.6 us (level)
  no operation moved by 1% of the time
where the time goes in v6:
time: 39.6 us; the launch traced here: 39.4 us
  Pallas kernels  38.1 us (96%)
  local copies, waits for them, and re-layouts  0.66 us (2%)
  between operations  0.64 us (2%)
    pallas_call x1, Pallas kernels, body(): pl.pallas_call(functools.partial(kernel, nx, ny, rows, cols), out_shape=s...  38.1 us

profile of v6, /device:TPU:1, one launch (start us, length us, event | category | flops | bytes accessed | tf_op | source)
XLA Modules:
  0.0 39.4 jit_solution(12576119940893547432)
XLA Ops:
  0.6 38.1 %shard_map.77 = f32[2,4,16,256]{3,2,1,0:T(8,128)S(1)} custom-call(f32[4,16,256]{2,1,0:T(8,128)} %guess.1, f32[3,4,512]{2,1,0:T(4,128)} %velocity.1, f32[4,512]{1,0:T(4,128)} %leaf.1, s32[4,512]{1,0:T(4,128)} %canopy.1, s32[4,512]{1,0:T(4,128)} %solid.1, s32[8]{0:T(128)} %receptors.1), custom_call_target="tpu_custom_call" | custom-call | tf_op jit(solution)/shard_map/pallas_call | solution.py:492
  38.8 0.7 %slice_bitcast_fusion = (f32[4,16,256]{2,1,0:T(8,128)}, f32[4,16,256]{2,1,0:T(8,128)}) fusion(f32[2,4,16,256]{3,2,1,0:T(8,128)S(1)} %shard_map.77), kind=kLoop, calls=%fused_computation | loop fusion | bytes 262144 | tf_op jit(solution)/shard_map/squeeze | solution.py:525

commit v7 on v6

--- a/solution.py
+++ b/solution.py
@@ -260,7 +260,6 @@
     expand(middle_cells)
     arrive([moving_0[n] for n in slanted])
     expand([cell for cell in all_cells if cell not in own_cells + middle_cells])
-    pass_y(1)
     arrive(moving_1)
     pass_x(1)
 
@@ -348,6 +347,7 @@
         advance(j, FIRST - 1 - j)
     moving_2 = exchange(basis.at[FIRST - 1], 2, DEGREE + 1 - FIRST)
     depart(moving_2)
+    pass_y(1)
     for a in range(FIRST):
         products(a)
     stacked = [stack(block) for block in blocks if block[-1] and block[-1][0] < FIRST]

time: 39.6 us -> 39.6 us (level)
  no operation moved by 1% of the time
where the time goes in v7:
time: 39.6 us; the launch traced here: 39.4 us
  Pallas kernels  38.1 us (96%)
  local copies, waits for them, and re-layouts  0.66 us (2%)
  between operations  0.64 us (2%)
    pallas_call x1, Pallas kernels, body(): pl.pallas_call(functools.partial(kernel, nx, ny, rows, cols), out_shape=s...  38.1 us

profile of v7, /device:TPU:1, one launch (start us, length us, event | category | flops | bytes accessed | tf_op | source)
XLA Modules:
  0.0 39.4 jit_solution(13872129374010124805)
XLA Ops:
  0.6 38.1 %shard_map.77 = f32[2,4,16,256]{3,2,1,0:T(8,128)S(1)} custom-call(f32[4,16,256]{2,1,0:T(8,128)} %guess.1, f32[3,4,512]{2,1,0:T(4,128)} %velocity.1, f32[4,512]{1,0:T(4,128)} %leaf.1, s32[4,512]{1,0:T(4,128)} %canopy.1, s32[4,512]{1,0:T(4,128)} %solid.1, s32[8]{0:T(128)} %receptors.1), custom_call_target="tpu_custom_call" | custom-call | tf_op jit(solution)/shard_map/pallas_call | solution.py:492
  38.7 0.7 %slice_bitcast_fusion = (f32[4,16,256]{2,1,0:T(8,128)}, f32[4,16,256]{2,1,0:T(8,128)}) fusion(f32[2,4,16,256]{3,2,1,0:T(8,128)S(1)} %shard_map.77), kind=kLoop, calls=%fused_computation | loop fusion | bytes 262144 | tf_op jit(solution)/shard_map/squeeze | solution.py:525
